TPU v7x, 128 devices: a whole 4x4x4 slice. The times are simulated.
128 devices in a mesh: req: 32 (over y, x, core), kv: 4 (over z).
Axes of the slice: x: 4, y: 4, z: 4, core: 2. Of those that a mesh axis runs over, the one named last changes fastest.
Arguments:
- tokens: bfloat16 [4096, 2048], P('req'), may hold values from -6 to 6
- lengths: int32 [4096], replicated, may hold values from 1 to 1024, as said below
- page_table: int32 [4096, 16], P('req'), may hold values from 0 to 367, as said below
- key_cache: bfloat16 [11776, 4, 64, 128], P('req', 'kv'), may hold values from -320 to 320
- value_page_cache: bfloat16 [11776, 4, 64, 128], P('req', 'kv'), may hold values from -6 to 6
- mig_slot: int32 [32, 2], replicated, may hold values from 0 to 127, as said below
- attn_gain: float32 [2048], replicated, may hold values from 0.1 to 1.9
- w_query: bfloat16 [2048, 4096], P(None, 'kv'), may hold values from -0.125 to 0.125
- key_weight: bfloat16 [2048, 512], P(None, 'kv'), may hold values from -0.125 to 0.125
- value_weight: bfloat16 [2048, 512], P(None, 'kv'), may hold values from -0.125 to 0.125
- w_out: bfloat16 [4096, 2048], P('kv'), may hold values from -0.09375 to 0.09375
- moe_gain: float32 [2048], replicated, may hold values from 0.1 to 1.9
- routes: int32 [4096, 8], P(('req', 'kv')), may hold values from 0 to 127, all different within a row; in each aligned block of 32 rows (0 to 31, 32 to 63, ...) at most 4 rows name the same one
- gate_probs: float32 [4096, 8], P(('req', 'kv')), may hold values from 0.05 to 1
- w_gate: bfloat16 [128, 2048, 768], P(('req', 'kv')), may hold values from -0.125 to 0.125
- w_up: bfloat16 [128, 2048, 768], P(('req', 'kv')), may hold values from -0.125 to 0.125
- w_down: bfloat16 [128, 768, 2048], P(('req', 'kv')), may hold values from -0.21875 to 0.21875
Outputs:
- layer_out: bfloat16 [4096, 2048], P(('req', 'kv'))
- moved_keys: bfloat16 [64, 4, 1024, 128], P('req', 'kv')
- moved_values: bfloat16 [64, 4, 1024, 128], P('req', 'kv')
Inputs may be any that keep to these rules, and one draw needn't show every extreme that they name: `lengths`: in each block of 128 requests of one index of req, between 2 and 16 requests are longer than 64 tokens and the others are at most 64 long; some request is exactly 1024 long. `page_table`: entries j below the ceiling of lengths[r] / 64 name distinct pages of the pool of request r's own index of req, counted within that pool; later entries are arbitrary pages of that pool. `mig_slot`: row g names 2 distinct local rows of index g of req, each a request longer than 64 tokens. `routes`: in the rows of one device (aligned blocks of 32 rows) no expert is named by more than 4 rows.
All inputs are finite; a program needn't handle non-finite values.
Results may differ from a plain program's by a relative error of at most 0.011.
Values may be sent and summed in bfloat16 or wider, within the bound.
No kernel may reach another device: no remote copies, remote signals or barrier semaphores. Data moves between devices by JAX's collectives and lax.ppermute only.
A program may use at most 128 MiB of HBM per device.

v0:
```python
import math
import jax
import jax.numpy as jnp
from jax import lax
from jax.sharding import PartitionSpec as P

EPSILON = 1e-06
THETA = 1000000.0


def from_behind(shard, axis, by):
    size = lax.axis_size(axis)
    return lax.ppermute(shard, axis, [(i, (i + by) % size) for i in range(size)])


def rms_scale(inputs, gain_vec):
    return (
        inputs * lax.rsqrt(jnp.mean(inputs * inputs, axis=-1, keepdims=True) + EPSILON) * gain_vec
    )


def rotate(vectors, positions):
    half_width = vectors.shape[-1] // 2
    exponent = jnp.arange(half_width, dtype=jnp.float32) * (-2.0 / vectors.shape[-1])
    angles = positions.astype(jnp.float32)[..., None] * THETA**exponent
    cosine = jnp.cos(angles)
    sine_part = jnp.sin(angles)
    front_half = vectors[..., :half_width]
    back_half = vectors[..., half_width:]
    return jnp.concatenate(
        [front_half * cosine - back_half * sine_part, back_half * cosine + front_half * sine_part],
        axis=-1,
    )


def project(token_rows, attn_gain, w_query, key_weight, value_weight, positions):
    normalized_rows = rms_scale(token_rows.astype(jnp.float32), attn_gain).astype(jnp.bfloat16)
    head_size = key_weight.shape[1]
    queries = jnp.dot(normalized_rows, w_query, preferred_element_type=jnp.float32).reshape(
        token_rows.shape[0], -1, head_size
    )
    fresh_key = jnp.dot(normalized_rows, key_weight, preferred_element_type=jnp.float32)
    fresh_value = jnp.dot(normalized_rows, value_weight, preferred_element_type=jnp.float32).astype(
        jnp.bfloat16
    )
    queries = rotate(rms_scale(queries, 1.0), positions[:, None]).astype(jnp.bfloat16)
    fresh_key = rotate(rms_scale(fresh_key, 1.0), positions).astype(jnp.bfloat16)
    return (queries, fresh_key, fresh_value)


def pool_pages(page_table, lengths_here, pool_size, page_len):
    requests_here, max_pages = page_table.shape
    counts = (lengths_here + page_len - 1) // page_len
    matched = (page_table[:, :, None] == jnp.arange(pool_size)[None, None, :]) & (
        jnp.arange(max_pages)[None, :, None] < counts[:, None, None]
    )
    owned_by = jnp.any(matched, axis=1)
    in_use = jnp.any(owned_by, axis=0)
    owners = jnp.sum(
        owned_by.astype(jnp.int32) * jnp.arange(requests_here, dtype=jnp.int32)[:, None], axis=0
    )
    page_pos = jnp.sum(
        matched.astype(jnp.int32) * jnp.arange(max_pages, dtype=jnp.int32)[None, :, None],
        axis=(0, 1),
    )
    return (owners, page_pos, in_use)


def attend(queries, key_self, value_self, page_sets, lengths_here):
    head_size = queries.shape[-1]
    scale_factor = 1.0 / math.sqrt(head_size)
    requests_here = queries.shape[0]
    self_score = (
        jnp.einsum("rgh,rh->rg", queries, key_self, preferred_element_type=jnp.float32)
        * scale_factor
    )
    best_score = self_score
    prepared = []
    for page_keys, page_values, owners, page_pos, in_use in page_sets:
        page_len = page_keys.shape[1]
        member = (owners[:, None] == jnp.arange(requests_here)[None, :]) & in_use[:, None]
        page_queries = jnp.take(queries, owners, axis=0)
        scores = (
            jnp.einsum("pgh,pth->pgt", page_queries, page_keys, preferred_element_type=jnp.float32)
            * scale_factor
        )
        position = page_pos[:, None] * page_len + jnp.arange(page_len)[None, :]
        usable = (position < jnp.take(lengths_here, owners)[:, None]) & in_use[:, None]
        page_best = jnp.max(jnp.where(usable[:, None, :], scores, -jnp.inf), axis=2)
        best_score = jnp.maximum(
            best_score,
            jnp.max(jnp.where(member[:, :, None], page_best[:, None, :], -jnp.inf), axis=0),
        )
        prepared.append((scores, usable, member, owners, page_values))
    self_weight = jnp.exp(self_score - best_score)
    rounded_self = lax.optimization_barrier(self_weight.astype(jnp.bfloat16)).astype(jnp.float32)
    denominator = self_weight
    summed = rounded_self[:, :, None] * value_self.astype(jnp.float32)[:, None, :]
    for scores, usable, member, owners, page_values in prepared:
        shifted = scores - jnp.take(best_score, owners, axis=0)[:, :, None]
        weights = jnp.where(usable[:, None, :], jnp.exp(jnp.minimum(shifted, 0.0)), 0.0)
        selector = member.astype(jnp.float32)
        denominator = denominator + jnp.dot(
            selector.T, jnp.sum(weights, axis=2), precision=lax.Precision.HIGHEST
        )
        page_out = jnp.einsum(
            "pgt,pth->pgh",
            weights.astype(jnp.bfloat16),
            page_values,
            preferred_element_type=jnp.float32,
        )
        summed = summed + jnp.dot(
            selector.T, page_out.reshape(page_out.shape[0], -1), precision=lax.Precision.HIGHEST
        ).reshape(summed.shape)
    return (summed / denominator[:, :, None]).reshape(requests_here, -1).astype(jnp.bfloat16)


def body(
    tokens,
    lengths,
    page_table,
    key_cache,
    value_page_cache,
    mig_slot,
    attn_gain,
    w_query,
    key_weight,
    value_weight,
    w_out,
    moe_gain,
    routes,
    gate_probs,
    w_gate,
    w_up,
    w_down,
):
    req_count = lax.axis_size("req")
    kv_count = lax.axis_size("kv")
    req_here = lax.axis_index("req")
    kv_here = lax.axis_index("kv")
    requests_here, model_width = tokens.shape
    pool_size = key_cache.shape[0]
    page_len = key_cache.shape[2]
    max_pages = page_table.shape[1]
    migrants = mig_slot.shape[1]
    max_len = max_pages * page_len
    partner = (req_here + req_count // 2) % req_count
    own_lengths = lax.dynamic_slice_in_dim(lengths, req_here * requests_here, requests_here)
    own_slots = lax.dynamic_index_in_dim(mig_slot, req_here, 0, keepdims=False)
    partner_slots = lax.dynamic_index_in_dim(mig_slot, partner, 0, keepdims=False)
    partner_lengths = jnp.take(
        lax.dynamic_slice_in_dim(lengths, partner * requests_here, requests_here), partner_slots
    )
    post_lengths = own_lengths.at[own_slots].set(partner_lengths)
    pool_keys = key_cache[:, 0]
    pool_values = value_page_cache[:, 0]
    owners, page_pos, in_use = pool_pages(page_table, own_lengths, pool_size, page_len)
    depart_pages = jnp.take(page_table, own_slots, axis=0)
    depart_mask = jnp.arange(max_len)[None, :] < jnp.take(own_lengths, own_slots)[:, None]
    depart_keys = jnp.where(
        depart_mask[:, :, None],
        jnp.take(pool_keys, depart_pages, axis=0).reshape(migrants, max_len, -1),
        jnp.zeros((), jnp.bfloat16),
    )
    depart_values = jnp.where(
        depart_mask[:, :, None],
        jnp.take(pool_values, depart_pages, axis=0).reshape(migrants, max_len, -1),
        jnp.zeros((), jnp.bfloat16),
    )
    leaving_tokens = jnp.take(tokens, own_slots, axis=0)
    arrived_keys, arrived_values, arrived_tokens = from_behind(
        (depart_keys, depart_values, leaving_tokens), "req", req_count // 2
    )
    settled_tokens = tokens.at[own_slots].set(arrived_tokens)
    queries, fresh_key, fresh_value = project(
        settled_tokens, attn_gain, w_query, key_weight, value_weight, post_lengths
    )
    staying = in_use & jnp.logical_not(jnp.any(owners[:, None] == own_slots[None, :], axis=1))
    arrival_set = (
        arrived_keys.reshape(migrants * max_pages, page_len, -1),
        arrived_values.reshape(migrants * max_pages, page_len, -1),
        jnp.repeat(own_slots, max_pages),
        jnp.tile(jnp.arange(max_pages, dtype=jnp.int32), migrants),
        jnp.ones((migrants * max_pages,), jnp.bool_),
    )
    attended = attend(
        queries,
        fresh_key,
        fresh_value,
        [(pool_keys, pool_values, owners, page_pos, staying), arrival_set],
        post_lengths,
    )
    disp_rows = requests_here // kv_count
    totals = lax.psum(
        jnp.dot(attended, w_out, preferred_element_type=jnp.float32).astype(jnp.bfloat16), "kv"
    ).astype(jnp.float32)
    projected = lax.dynamic_slice_in_dim(totals, kv_here * disp_rows, disp_rows)
    residual_rows = lax.dynamic_slice_in_dim(settled_tokens, kv_here * disp_rows, disp_rows).astype(
        jnp.float32
    )
    hidden = (residual_rows + projected).astype(jnp.bfloat16)
    moe_in = rms_scale(hidden.astype(jnp.float32), moe_gain).astype(jnp.bfloat16)
    devices = req_count * kv_count
    local_experts = w_gate.shape[0]
    expert_total = devices * local_experts
    top_count = routes.shape[1]
    capacity = max(2, 2 * disp_rows * top_count // expert_total)
    flat_routes = routes.reshape(-1)
    expert_hot = (
        flat_routes[:, None] == jnp.arange(expert_total, dtype=jnp.int32)[None, :]
    ).astype(jnp.int32)
    ranking = jnp.sum((jnp.cumsum(expert_hot, axis=0) - expert_hot) * expert_hot, axis=1)
    slot_index = flat_routes * capacity + ranking
    placement = (
        jnp.arange(expert_total * capacity, dtype=jnp.int32)[:, None] == slot_index[None, :]
    ).reshape(expert_total * capacity, disp_rows, top_count)
    placement = jnp.any(placement, axis=2).astype(jnp.bfloat16)
    outgoing = jnp.dot(placement, moe_in, preferred_element_type=jnp.float32).astype(jnp.bfloat16)
    outgoing = outgoing.reshape(devices, local_experts, capacity, model_width)
    received = lax.all_to_all(outgoing, ("req", "kv"), split_axis=0, concat_axis=0, tiled=True)
    gate_part = jnp.einsum("sexd,edf->sexf", received, w_gate, preferred_element_type=jnp.float32)
    up_part = jnp.einsum("sexd,edf->sexf", received, w_up, preferred_element_type=jnp.float32)
    activated = (jax.nn.silu(gate_part) * up_part).astype(jnp.bfloat16)
    returned = lax.all_to_all(
        jnp.einsum("sexf,efd->sexd", activated, w_down, preferred_element_type=jnp.float32).astype(
            jnp.bfloat16
        ),
        ("req", "kv"),
        split_axis=0,
        concat_axis=0,
        tiled=True,
    )
    picked = jnp.take(returned.reshape(-1, model_width), slot_index, axis=0).reshape(
        disp_rows, top_count, model_width
    )
    shares = gate_probs / jnp.sum(gate_probs, axis=1, keepdims=True)
    mixed_rows = hidden.astype(jnp.float32) + jnp.sum(
        shares[:, :, None] * picked.astype(jnp.float32), axis=1
    )
    return (mixed_rows.astype(jnp.bfloat16), arrived_keys[:, None], arrived_values[:, None])


def solution(mesh):
    in_specs = (
        P("req", None),
        P(),
        P("req", None),
        P("req", "kv", None, None),
        P("req", "kv", None, None),
        P(),
        P(),
        P(None, "kv"),
        P(None, "kv"),
        P(None, "kv"),
        P("kv", None),
        P(),
        P(("req", "kv"), None),
        P(("req", "kv"), None),
        P(("req", "kv"), None, None),
        P(("req", "kv"), None, None),
        P(("req", "kv"), None, None),
    )
    out_specs = (P(("req", "kv"), None), P("req", "kv", None, None), P("req", "kv", None, None))
    return jax.shard_map(body, mesh=mesh, in_specs=in_specs, out_specs=out_specs, check_vma=False)
```

profile of v0, /device:TPU:1, one launch (start us, length us, event | category | flops | bytes accessed | tf_op | source)
XLA Modules:
  0.0 262.2 jit_solution(586046590555309745)
XLA Ops:
  7.2 2.0 copy.167
  9.3 1.0 dynamic-slice_reduce_fusion
  10.3 0.8 and_select_fusion.1
  11.1 0.6 gather_fusion.10
  11.7 1.7 gather_fusion
  13.5 3.8 %collective-permute-start = (bf16[2,2048]{1,0:T(2,128)(2,1)S(1)}, bf16[2,2048]{1,0:T(2,128)(2,1)S(1)}, u32[]{:S(2)}, u32[]{:S(2)}) collective-permute-start(bf16[2,2048]{1,0:T(2,128)(2,1)S(1)} %broadcast_select_fusion.3), channel_id=1, source_target_pairs={{0,64},{4,68},{8,72},{12,76},{16,80},{20,84},{24,88},{28,92},{32,9... | collective-permute-start | bytes 24584 | tf_op jit(solution)/shard_map/ppermute | solution.py:13
  17.3 0.8 copy.105
  18.1 0.6 gather_fusion.5
  18.8 4.1 %gather_fusion.12 = bf16[32,64,128]{2,1,0:T(8,128)(2,1)} fusion(bf16[368,64,128]{2,1,0:T(8,128)(2,1)} %bitcast.173, s32[1024]{0:T(1024)S(1)} %pad_clamp_fusion.1), kind=kCustom, calls=%fused_computation.3.clone | custom fusion | bytes 1048704 | tf_op jit(solution)/shard_map/jit(_take)/gather | solution.py:167
  22.9 4.1 %gather_fusion.11 = bf16[32,64,128]{2,1,0:T(8,128)(2,1)} fusion(bf16[368,64,128]{2,1,0:T(8,128)(2,1)} %bitcast.172, s32[1024]{0:T(1024)S(1)} %pad_clamp_fusion.1), kind=kCustom, calls=%fused_computation.1.clone | custom fusion | bytes 1048704 | tf_op jit(solution)/shard_map/jit(_take)/gather | solution.py:162
  27.1 1.4 broadcast_select_fusion
  28.5 1.3 bitcast_select_fusion.1
  29.9 3.0 %collective-permute-start.2 = (bf16[2,1024,128]{2,1,0:T(8,128)(2,1)}, bf16[2,1024,128]{2,1,0:T(8,128)(2,1)}, u32[]{:S(2)}, u32[]{:S(2)}) collective-permute-start(bf16[2,1024,128]{2,1,0:T(8,128)(2,1)} %get-tuple-element.32), channel_id=1, source_target_pairs={{0,64},{4,68},{8,72},{12,76},{16,80},{20,84},{24,88},{28,92},{32,9... | collective-permute-start | bytes 1572872 | tf_op jit(solution)/shard_map/ppermute | solution.py:13
  33.6 0.7 select_reduce_fusion
  34.5 0.6 gather_fusion.9
  35.1 0.6 scatter_fusion.1
  35.8 2.7 %gather_fusion.1 = s32[368]{0:T(512)S(1)} fusion(s32[128]{0:T(128)S(1)} %scatter_fusion.1, s32[1024]{0:T(1024)S(1)} %pad_clamp_fusion.4), kind=kCustom, calls=%fused_computation.5 | custom fusion | bytes 4416 | tf_op jit(solution)/shard_map/jit(_take)/gather | solution.py:88
  39.0 0.8 fusion.64
  39.8 0.7 gather_fusion.3
  40.5 0.7 iota_compare_fusion.4
  42.3 0.6 copy-done.7
  43.3 2.5 scatter_fusion
  45.8 1.2 fusion.47
  47.1 3.1 %convolution_bitcast_fusion = f32[16,8,8,128]{3,1,2,0:T(8,128)S(1)} fusion(bf16[2048,1024]{1,0:T(8,128)(2,1)} %param.28, bf16[128,2048]{1,0:T(8,128)(2,1)} %scatter_fusion, f32[2048]{0:T(1024)S(1)} %copy-done.19, f32[128]{0:T(128)S(1)} %add_rsqrt_fusion.3), kind=kOutput, calls=%fused_computation.55 | convolution fusion | flops 537919488 | bytes 5251584 | tf_op jit(solution)/shard_map/dot_general | solution.py:39
  50.3 0.8 copy-done.2
  51.5 2.0 broadcast_multiply_fusion
  53.6 1.6 multiply_reduce_fusion.3
  55.7 1.4 subtract_convert_fusion
  57.2 0.9 multiply_reduce_fusion.1
  58.1 2.5 gather_fusion.2
  60.6 0.7 gather_fusion.4
  61.3 0.9 copy.124
  62.2 1.6 fusion.42
  63.8 0.7 copy.106
  64.5 7.4 %select_reduce_fusion.2 = (f32[368,8]{1,0:T(8,128)S(1)}, f32[368,8,64]{2,1,0:T(8,128)}) fusion(pred[368,64]{1,0:T(8,128)(4,1)S(1)} %fusion.65, bf16[368,1,64,128]{3,2,1,0:T(8,128)(2,1)} %param.24, bf16[368,8,128]{2,1,0:T(8,128)(2,1)} %gather_fusion.2, pred[368]{0:T(512)(128)(4,1)} %get-tuple-element.18), kind=kOutput, calls=%fused_computation.48 | convolution fusion | flops 49173632 | bytes 7572336 | tf_op jit(solution)/shard_map/pgh,pth->pgt/dot_general | solution.py:84
  72.4 1.6 select_reduce_fusion.5
  74.1 0.6 fusion.91
  75.3 1.3 gather_fusion.7
  76.6 1.2 gather_fusion.6
  77.9 0.9 broadcast_select_fusion.4
  78.8 0.7 broadcast_select_fusion.2
  79.5 2.3 fusion.40
  82.1 3.8 %fusion.51 = f32[368,8,128]{2,1,0:T(8,128)S(1)} fusion(f32[368,8,64]{2,1,0:T(8,128)S(1)} %copy-done.1, f32[368,8]{1,0:T(8,128)S(1)} %broadcast_select_fusion.2, pred[368,64]{1,0:T(8,128)(4,1)S(1)} %copy-done.6, bf16[368,1,64,128]{3,2,1,0:T(8,128)(2,1)} %param.25), kind=kOutput, calls=%fused_computation.70 | convolution fusion | flops 48988160 | bytes 8325632 | tf_op jit(solution)/shard_map/pgt,pth->pgh/dot_general | solution.py:106
  85.9 1.3 fusion.78
  88.0 1.6 fusion.35
  89.5 0.6 fusion.39
  90.2 1.5 convolution_convert_fusion.1
  92.5 41.7 %all-reduce.2.cloned.1.call-done = bf16[128,2048]{1,0:T(8,128)(2,1)} async-done(((bf16[128,2048]{1,0:T(8,128)(2,1)}), bf16[128,2048]{1,0:T(8,128)(2,1)}) %all-reduce.2.cloned.1.call-update) | async-done | bytes 524304 | tf_op jit(solution)/shard_map/psum | solution.py:194
  134.2 1.1 fusion.60
  135.3 2.1 convolution_convert_fusion
  137.5 4.1 %reshape.604 = bf16[128,1,4,2048]{3,2,0,1:T(4,128)(2,1)} reshape(bf16[512,2048]{1,0:T(8,128)(2,1)} %convolution_convert_fusion) | data formatting | bytes 4194304 | tf_op jit(solution)/shard_map/reshape | solution.py:219
  141.6 41.6 %all_to_all.10 = bf16[128,1,4,2048]{3,2,1,0:T(4,128)(2,1)S(1)} all-to-all(bf16[128,1,4,2048]{3,2,1,0:T(4,128)(2,1)} %bitcast.171), channel_id=1, replica_groups=mesh['req'=32,'kv'=4] {'req','kv'}, dimensions={0} | all-to-all | bytes 4194304 | tf_op jit(solution)/shard_map/all_to_all | solution.py:220
  183.2 1.3 copy-done.4
  184.5 4.8 %fusion.4 = f32[128,4,768]{2,0,1:T(8,128)} fusion(bf16[1,2048,768]{2,1,0:T(8,128)(2,1)S(1)} %copy-done.32, bf16[128,1,4,2048]{3,2,1,0:T(4,128)(2,1)S(1)} %all_to_all.10), kind=kOutput, calls=%fused_computation.19 | convolution fusion | flops 1610612736 | bytes 6815744 | tf_op jit(solution)/shard_map/sexd,edf->sexf/dot_general | solution.py:221
  189.3 9.9 %fusion.12 = bf16[128,1,4,2048]{3,0,2,1:T(8,128)(2,1)} fusion(bf16[1,768,2048]{2,1,0:T(8,128)(2,1)S(1)} %copy-done, bf16[1,2048,768]{2,1,0:T(8,128)(2,1)} %param.36, bf16[128,1,4,2048]{3,2,1,0:T(4,128)(2,1)} %copy-done.4, f32[128,4,768]{2,0,1:T(8,128)} %fusion.4), kind=kOutput, calls=%fused_computation.28 | convolution fusion | flops 3224633344 | bytes 12058624 | tf_op jit(solution)/shard_map/sexf,efd->sexd/dot_general | solution.py:225
  199.2 4.5 %copy.119 = bf16[128,1,4,2048]{3,2,1,0:T(4,128)(2,1)} copy(bf16[128,1,4,2048]{3,0,2,1:T(8,128)(2,1)} %fusion.12) | data formatting | bytes 4194304 | tf_op jit(solution)/shard_map/convert_element_type | solution.py:225
  203.7 5.1 %all-to-all-start.1 = ((bf16[128,1,4,2048]{3,2,1,0:T(4,128)(2,1)}), bf16[128,1,4,2048]{3,2,1,0:T(4,128)(2,1)}, u32[]{:S(2)}, u32[]{:S(2)}) async-start(bf16[128,1,4,2048]{3,2,1,0:T(4,128)(2,1)} %copy.119), calls=%async_computation.1 | async-start | bytes 4194304 | tf_op jit(solution)/shard_map/all_to_all | solution.py:224
  209.0 29.8 %all-to-all-done.1 = bf16[128,1,4,2048]{3,2,1,0:T(4,128)(2,1)} async-done(((bf16[128,1,4,2048]{3,2,1,0:T(4,128)(2,1)}), bf16[128,1,4,2048]{3,2,1,0:T(4,128)(2,1)}, u32[]{:S(2)}, u32[]{:S(2)}) %all-to-all-start.1) | async-done | bytes 2097184 | tf_op jit(solution)/shard_map/all_to_all | solution.py:224
  238.9 4.0 %reshape.610 = bf16[512,2048]{1,0:T(8,128)(2,1)} reshape(bf16[128,1,4,2048]{3,2,1,0:T(4,128)(2,1)} %all-to-all-done.1) | data formatting | bytes 4194304 | tf_op jit(solution)/shard_map/reshape | solution.py:233
  242.8 5.2 %gather_fusion.8 = bf16[256,2048]{1,0:T(8,128)(2,1)} fusion(bf16[512,2048]{1,0:T(8,128)(2,1)} %reshape.610, s32[1024]{0:T(1024)S(1)} %pad_clamp_fusion), kind=kCustom, calls=%fused_computation.12 | custom fusion | bytes 2098176 | tf_op jit(solution)/shard_map/jit(_take)/gather | solution.py:233
  248.0 2.9 %multiply_reduce_fusion = f32[32,2048]{1,0:T(8,128)S(1)} fusion(bf16[256,2048]{1,0:T(8,128)(2,1)} %gather_fusion.8, f32[32,8]{1,0:T(8,128)S(1)} %copy.111, pred[32,8]{1,0:T(8,128)(4,1)S(1)} %get-tuple-element.9), kind=kLoop, calls=%fused_computation.32 | loop fusion | flops 2031616 | bytes 1312000 | tf_op jit(solution)/shard_map/reduce_sum | solution.py:237
  250.9 0.7 fusion.63
  251.6 1.9 copy.168
  253.5 1.9 copy.169
  (146 shorter events, 7.4 us)
Async XLA Ops:
  7.2 182.1 %copy-start = (bf16[1,768,2048]{2,1,0:T(8,128)(2,1)S(1)}, bf16[1,768,2048]{2,1,0:T(8,128)(2,1)}, u32[]{:S(2)}) copy-start(bf16[1,768,2048]{2,1,0:T(8,128)(2,1)} %param.37) | copy-start | bytes 9437188
  7.2 127.0 %all-reduce.2.cloned.1.call-start = ((), (), s32[]{:S(2)}) async-start(), calls=%async_computation.2 | async-start | bytes 1048576 | tf_op jit(solution)/shard_map/psum | solution.py:194
  13.5 29.8 %collective-permute-start = (bf16[2,2048]{1,0:T(2,128)(2,1)S(1)}, bf16[2,2048]{1,0:T(2,128)(2,1)S(1)}, u32[]{:S(2)}, u32[]{:S(2)}) collective-permute-start(bf16[2,2048]{1,0:T(2,128)(2,1)S(1)} %broadcast_select_fusion.3), channel_id=1, source_target_pairs={{0,64},{4,68},{8,72},{12,76},{16,80},{20,84},{24,88},{28,92},{32,9... | collective-permute-start | bytes 24584 | tf_op jit(solution)/shard_map/ppermute | solution.py:13
  27.1 5.7 %copy-start.11 = (s32[128,16]{0,1:T(8,128)S(1)}, s32[128,16]{0,1:T(8,128)}, u32[]{:S(2)}) copy-start(s32[128,16]{0,1:T(8,128)} %param.23) | copy-start | bytes 24580
  29.8 42.6 %collective-permute-start.1 = (bf16[2,1024,128]{2,1,0:T(8,128)(2,1)}, bf16[2,1024,128]{2,1,0:T(8,128)(2,1)}, u32[]{:S(2)}, u32[]{:S(2)}) collective-permute-start(bf16[2,1024,128]{2,1,0:T(8,128)(2,1)} %get-tuple-element.33), channel_id=1, source_target_pairs={{0,64},{4,68},{8,72},{12,76},{16,80},{20,84},{24,88},{28,92},{32,9... | collective-permute-start | bytes 1572872 | tf_op jit(solution)/shard_map/ppermute | solution.py:13
  29.9 56.1 %collective-permute-start.2 = (bf16[2,1024,128]{2,1,0:T(8,128)(2,1)}, bf16[2,1024,128]{2,1,0:T(8,128)(2,1)}, u32[]{:S(2)}, u32[]{:S(2)}) collective-permute-start(bf16[2,1024,128]{2,1,0:T(8,128)(2,1)} %get-tuple-element.32), channel_id=1, source_target_pairs={{0,64},{4,68},{8,72},{12,76},{16,80},{20,84},{24,88},{28,92},{32,9... | collective-permute-start | bytes 1572872 | tf_op jit(solution)/shard_map/ppermute | solution.py:13
  34.5 6.7 %copy-start.28 = (s32[32]{0:T(128)}, s32[32]{0:T(128)S(1)}, u32[]{:S(2)}) copy-start(s32[32]{0:T(128)S(1)} %eq.110) | copy-start | bytes 388
  34.5 7.3 %copy-start.27 = (s32[32,8]{0,1:T(8,128)S(1)}, s32[32,8]{0,1:T(8,128)}, u32[]{:S(2)}) copy-start(s32[32,8]{0,1:T(8,128)} %param.33) | copy-start | bytes 3076
  35.7 11.3 %copy-start.19 = (f32[2048]{0:T(1024)S(1)}, f32[2048]{0:T(1024)}, u32[]{:S(2)}) copy-start(f32[2048]{0:T(1024)} %param.27) | copy-start | bytes 24580
  35.8 22.4 %copy-start.12 = (s32[1024]{0:T(1024)}, s32[1024]{0:T(1024)S(1)}, u32[]{:S(2)}) copy-start(s32[1024]{0:T(1024)S(1)} %pad_clamp_fusion.4) | copy-start | bytes 12292
  39.0 11.2 %copy-start.25 = (pred[368]{0:T(512)(128)(4,1)}, pred[368]{0:T(512)(128)(4,1)S(1)}, u32[]{:S(2)}) copy-start(pred[368]{0:T(512)(128)(4,1)S(1)} %not_and_fusion) | copy-start | bytes 1108
  39.8 1.9 copy-start.22
  42.3 0.7 copy-start.7
  43.2 21.4 %copy-start.5 = (pred[368,64]{1,0:T(8,128)(4,1)}, pred[368,64]{1,0:T(8,128)(4,1)S(1)}, u32[]{:S(2)}) copy-start(pred[368,64]{1,0:T(8,128)(4,1)S(1)} %fusion.65) | copy-start | bytes 70660
  43.3 6.9 %copy-start.24 = (s32[128,3]{0,1:T(4,128)}, s32[128,3]{0,1:T(4,128)S(1)}, u32[]{:S(2)}) copy-start(s32[128,3]{0,1:T(4,128)S(1)} %reduce-window.9) | copy-start | bytes 4612
  47.1 6.5 %copy-start.30 = (f32[128]{0:T(128)}, f32[128]{0:T(128)S(1)}, u32[]{:S(2)}) copy-start(f32[128]{0:T(128)S(1)} %add_rsqrt_fusion.3) | copy-start | bytes 1540
  50.3 0.8 copy-start.2
  55.7 6.5 %copy-start.31 = (f32[128]{0:T(128)S(1)}, f32[128]{0:T(128)}, u32[]{:S(2)}) copy-start(f32[128]{0:T(128)} %copy-done.30) | copy-start | bytes 1540
  62.2 11.9 %copy-start.14 = (f32[128,8]{0,1:T(8,128)}, f32[128,8]{0,1:T(8,128)S(1)}, u32[]{:S(2)}) copy-start(f32[128,8]{0,1:T(8,128)S(1)} %copy.124) | copy-start | bytes 12292
  64.5 7.4 %copy-start.10 = (pred[368,128]{1,0:T(8,128)(4,1)S(1)}, pred[368,128]{1,0:T(8,128)(4,1)}, u32[]{:S(2)}) copy-start(pred[368,128]{1,0:T(8,128)(4,1)} %fusion.64) | copy-start | bytes 141316
  64.5 7.9 %copy-start.23 = (pred[32]{0:T(512)(128)(4,1)S(1)}, pred[32]{0:T(512)(128)(4,1)}, u32[]{:S(2)}) copy-start(pred[32]{0:T(512)(128)(4,1)} %get-tuple-element.20) | copy-start | bytes 100
  64.5 9.5 %copy-start.18 = (pred[32,128]{1,0:T(8,128)(4,1)S(1)}, pred[32,128]{1,0:T(8,128)(4,1)}, u32[]{:S(2)}) copy-start(pred[32,128]{1,0:T(8,128)(4,1)} %iota_compare_fusion.4) | copy-start | bytes 12292
  74.7 0.6 copy-start.16
  77.8 4.2 %copy-start.1 = (f32[368,8,64]{2,1,0:T(8,128)S(1)}, f32[368,8,64]{2,1,0:T(8,128)}, u32[]{:S(2)}) copy-start(f32[368,8,64]{2,1,0:T(8,128)} %get-tuple-element.45) | copy-start | bytes 2260996
  77.9 4.2 %copy-start.6 = (pred[368,64]{1,0:T(8,128)(4,1)S(1)}, pred[368,64]{1,0:T(8,128)(4,1)}, u32[]{:S(2)}) copy-start(pred[368,64]{1,0:T(8,128)(4,1)} %copy-done.5) | copy-start | bytes 70660
  82.0 5.3 %copy-start.15 = (f32[128,8]{0,1:T(8,128)S(1)}, f32[128,8]{0,1:T(8,128)}, u32[]{:S(2)}) copy-start(f32[128,8]{0,1:T(8,128)} %copy-done.14) | copy-start | bytes 12292
  82.0 5.3 %copy-start.17 = (f32[128,8]{0,1:T(8,128)S(1)}, f32[128,8]{0,1:T(8,128)}, u32[]{:S(2)}) copy-start(f32[128,8]{0,1:T(8,128)} %copy-done.16) | copy-start | bytes 12292
  82.0 5.3 %copy-start.26 = (pred[368]{0:T(512)(128)(4,1)S(1)}, pred[368]{0:T(512)(128)(4,1)}, u32[]{:S(2)}) copy-start(pred[368]{0:T(512)(128)(4,1)} %copy-done.25) | copy-start | bytes 1108
  82.1 5.7 %copy-start.21 = (bf16[128,8]{0,1:T(8,128)(2,1)S(1)}, bf16[128,8]{0,1:T(8,128)(2,1)}, u32[]{:S(2)}) copy-start(bf16[128,8]{0,1:T(8,128)(2,1)} %get-tuple-element.13) | copy-start | bytes 6148
  82.1 5.7 %copy-start.29 = (s32[32]{0:T(128)S(1)}, s32[32]{0:T(128)}, u32[]{:S(2)}) copy-start(s32[32]{0:T(128)} %copy-done.28) | copy-start | bytes 388
  82.1 5.9 %copy-start.9 = (f32[128,128]{0,1:T(8,128)S(1)}, f32[128,128]{0,1:T(8,128)}, u32[]{:S(2)}) copy-start(f32[128,128]{0,1:T(8,128)} %copy.106) | copy-start | bytes 196612
  87.8 2.4 copy-start.3
  90.2 1.6 slice-start
  90.2 1.6 copy-start.8
  90.2 45.1 %copy-start.20 = (f32[2048]{0:T(1024)S(1)}, f32[2048]{0:T(1024)}, u32[]{:S(2)}) copy-start(f32[2048]{0:T(1024)} %param.32) | copy-start | bytes 24580
  141.6 42.9 %copy-start.32 = (bf16[1,2048,768]{2,1,0:T(8,128)(2,1)S(1)}, bf16[1,2048,768]{2,1,0:T(8,128)(2,1)}, u32[]{:S(2)}) copy-start(bf16[1,2048,768]{2,1,0:T(8,128)(2,1)} %param.35) | copy-start | bytes 9437188
  183.2 1.3 copy-start.4
  203.7 5.2 %copy-start.13 = (f32[32,8]{0,1:T(8,128)S(1)}, f32[32,8]{0,1:T(8,128)}, u32[]{:S(2)}) copy-start(f32[32,8]{0,1:T(8,128)} %param.34) | copy-start | bytes 3076
  203.7 35.2 %all-to-all-start.1 = ((bf16[128,1,4,2048]{3,2,1,0:T(4,128)(2,1)}), bf16[128,1,4,2048]{3,2,1,0:T(4,128)(2,1)}, u32[]{:S(2)}, u32[]{:S(2)}) async-start(bf16[128,1,4,2048]{3,2,1,0:T(4,128)(2,1)} %copy.119), calls=%async_computation.1 | async-start | bytes 4194304 | tf_op jit(solution)/shard_map/all_to_all | solution.py:224
Sparse Core Ops, SparseCore 0:
  91.9 42.2 all-reduce.1
where the time goes:
time: 263 us; the launch traced here: 262 us
  waiting for transfers between devices  71.6 us (27%)
  local copies, waits for them, and re-layouts  55.9 us (21%)
  matrix products  41.6 us (16%)
  blocking collectives  41.6 us (16%)
  other arithmetic  24.9 us (9%)
  between operations  14.7 us (6%)
  starting transfers between devices  11.9 us (5%)
    psum x1, waiting for transfers between devices, body(): lax.psum(jnp.dot(attended, w_out, preferred_element_type=jnp.float32).ast...  41.7 us
    all_to_all x1, blocking collectives, body(): lax.all_to_all(outgoing, ('req', 'kv'), split_axis=0, concat_axis=0, tile...  41.6 us
    all_to_all x1, waiting for transfers between devices, body(): lax.all_to_all(jnp.einsum('sexf,efd->sexd', activated, w_down, preferred_...  29.8 us
    unnamed x74, local copies, waits for them, and re-layouts  10.2 us
    dot_general x1, matrix products, body(): jnp.einsum('sexf,efd->sexd', activated, w_down, preferred_element_type=jn...  9.86 us
    dot_general x2, matrix products, attend(): jnp.einsum('pgh,pth->pgt', page_queries, page_keys, preferred_element_typ...  8.98 us
    ppermute x3, starting transfers between devices, from_behind(): lax.ppermute(shard, axis, [(i, (i + by) % size) for i in range(size)])  6.78 us
  transfers between devices with their start and end apart: 5, of which 2 were waited for; matrix products, arithmetic and copies ran while one was open for 24% of the time, Pallas kernels for 0%

commit v1 on v0

--- a/solution.py
+++ b/solution.py
@@ -191,8 +191,11 @@
         post_lengths,
     )
     disp_rows = requests_here // kv_count
-    totals = lax.psum(
-        jnp.dot(attended, w_out, preferred_element_type=jnp.float32).astype(jnp.bfloat16), "kv"
+    totals = jnp.sum(
+        lax.all_gather(
+            jnp.dot(attended, w_out, preferred_element_type=jnp.float32).astype(jnp.bfloat16), "kv"
+        ),
+        axis=0,
     ).astype(jnp.float32)
     projected = lax.dynamic_slice_in_dim(totals, kv_here * disp_rows, disp_rows)
     residual_rows = lax.dynamic_slice_in_dim(settled_tokens, kv_here * disp_rows, disp_rows).astype(

time: 263 us -> 251 us (0.954)
  waiting for transfers between devices: 71.6 us -> 60.7 us
  blocking collectives: 41.6 us -> 38.9 us
    psum x1 -> x0, waiting for transfers between devices: 41.7 us -> none  [body(): lax.psum(jnp.dot(attended, w_out, preferred_element_type=jnp.float32).ast...]
    all_gather x0 -> x1, waiting for transfers between devices: none -> 30.8 us  [body(): lax.all_gather(jnp.dot(attended, w_out, preferred_element_type=jnp.float3...]
    reduce_sum x0 -> x1, other arithmetic: none -> 2.92 us  [body(): jnp.sum(lax.all_gather(jnp.dot(attended, w_out, preferred_element_type=jn...]
    all_to_all x1, blocking collectives: 41.6 us -> 38.9 us  [body(): lax.all_to_all(outgoing, ('req', 'kv'), split_axis=0, concat_axis=0, tile...]
    unnamed x74 -> x66, local copies, waits for them, and re-layouts: 10.2 us -> 9.54 us
  transfers between devices with their start and end apart: 5 -> 5, of which waited for: 2 -> 2; matrix products, arithmetic and copies ran while one was open for 24% -> 25% of each run, Pallas kernels for 0% -> 0%
where the time goes in v1:
time: 251 us; the launch traced here: 250 us
  waiting for transfers between devices  60.7 us (24%)
  local copies, waits for them, and re-layouts  54.5 us (22%)
  matrix products  41.6 us (17%)
  blocking collectives  38.9 us (15%)
  other arithmetic  27.3 us (11%)
  between operations  14.7 us (6%)
  starting transfers between devices  11.9 us (5%)
    all_to_all x1, blocking collectives, body(): lax.all_to_all(outgoing, ('req', 'kv'), split_axis=0, concat_axis=0, tile...  38.9 us
    all_gather x1, waiting for transfers between devices, body(): lax.all_gather(jnp.dot(attended, w_out, preferred_element_type=jnp.float3...  30.8 us
    all_to_all x1, waiting for transfers between devices, body(): lax.all_to_all(jnp.einsum('sexf,efd->sexd', activated, w_down, preferred_...  29.8 us
    dot_general x1, matrix products, body(): jnp.einsum('sexf,efd->sexd', activated, w_down, preferred_element_type=jn...  9.86 us
    unnamed x66, local copies, waits for them, and re-layouts  9.54 us
    dot_general x2, matrix products, attend(): jnp.einsum('pgh,pth->pgt', page_queries, page_keys, preferred_element_typ...  8.98 us
    ppermute x3, starting transfers between devices, from_behind(): lax.ppermute(shard, axis, [(i, (i + by) % size) for i in range(size)])  6.78 us
    gather x1, local copies, waits for them, and re-layouts, body(): jnp.take(returned.reshape(-1, model_width), slot_index, axis=0)  5.21 us
  transfers between devices with their start and end apart: 5, of which 2 were waited for; matrix products, arithmetic and copies ran while one was open for 25% of the time, Pallas kernels for 0%

profile of v1, /device:TPU:1, one launch (start us, length us, event | category | flops | bytes accessed | tf_op | source)
XLA Modules:
  0.0 249.6 jit_solution(13943218019710830984)
XLA Ops:
  7.2 2.0 copy.166
  9.3 1.0 dynamic-slice_reduce_fusion
  10.3 0.8 and_select_fusion.1
  11.1 0.6 gather_fusion.10
  11.7 1.7 gather_fusion
  13.5 3.8 %collective-permute-start = (bf16[2,2048]{1,0:T(2,128)(2,1)S(1)}, bf16[2,2048]{1,0:T(2,128)(2,1)S(1)}, u32[]{:S(2)}, u32[]{:S(2)}) collective-permute-start(bf16[2,2048]{1,0:T(2,128)(2,1)S(1)} %broadcast_select_fusion.3), channel_id=1, source_target_pairs={{0,64},{4,68},{8,72},{12,76},{16,80},{20,84},{24,88},{28,92},{32,9... | collective-permute-start | bytes 24584 | tf_op jit(solution)/shard_map/ppermute | solution.py:13
  17.3 0.8 copy.105
  18.8 4.1 %gather_fusion.12 = bf16[32,64,128]{2,1,0:T(8,128)(2,1)} fusion(bf16[368,64,128]{2,1,0:T(8,128)(2,1)} %bitcast.174, s32[1024]{0:T(1024)S(1)} %pad_clamp_fusion.1), kind=kCustom, calls=%fused_computation.3.clone | custom fusion | bytes 1048704 | tf_op jit(solution)/shard_map/jit(_take)/gather | solution.py:167
  22.9 4.1 %gather_fusion.11 = bf16[32,64,128]{2,1,0:T(8,128)(2,1)} fusion(bf16[368,64,128]{2,1,0:T(8,128)(2,1)} %bitcast.173, s32[1024]{0:T(1024)S(1)} %pad_clamp_fusion.1), kind=kCustom, calls=%fused_computation.1.clone | custom fusion | bytes 1048704 | tf_op jit(solution)/shard_map/jit(_take)/gather | solution.py:162
  27.1 1.4 broadcast_select_fusion
  28.5 1.3 bitcast_select_fusion.1
  29.9 3.0 %collective-permute-start.2 = (bf16[2,1024,128]{2,1,0:T(8,128)(2,1)}, bf16[2,1024,128]{2,1,0:T(8,128)(2,1)}, u32[]{:S(2)}, u32[]{:S(2)}) collective-permute-start(bf16[2,1024,128]{2,1,0:T(8,128)(2,1)} %get-tuple-element.32), channel_id=1, source_target_pairs={{0,64},{4,68},{8,72},{12,76},{16,80},{20,84},{24,88},{28,92},{32,9... | collective-permute-start | bytes 1572872 | tf_op jit(solution)/shard_map/ppermute | solution.py:13
  33.6 0.7 select_reduce_fusion
  34.5 0.6 gather_fusion.9
  35.1 0.6 scatter_fusion.1
  35.8 2.7 %gather_fusion.1 = s32[368]{0:T(512)S(1)} fusion(s32[128]{0:T(128)S(1)} %scatter_fusion.1, s32[1024]{0:T(1024)S(1)} %pad_clamp_fusion.4), kind=kCustom, calls=%fused_computation.5 | custom fusion | bytes 4416 | tf_op jit(solution)/shard_map/jit(_take)/gather | solution.py:88
  38.4 0.6 broadcast_select_fusion.5
  39.1 0.8 fusion.64
  39.9 0.7 gather_fusion.3
  40.6 0.6 broadcast_select_fusion.7
  41.6 2.5 %scatter_fusion = bf16[128,2048]{1,0:T(8,128)(2,1)} fusion(bf16[128,2048]{1,0:T(8,128)(2,1)} %copy.166, s32[2]{0:T(128)S(1)} %fusion.92, bf16[2,2048]{1,0:T(2,128)(2,1)S(1)} %collective-permute-done), kind=kCustom, calls=%fused_computation.13 | custom fusion | bytes 24584 | tf_op jit(solution)/shard_map/scatter | solution.py:174
  44.2 1.2 fusion.47
  45.4 3.1 %convolution_bitcast_fusion = f32[16,8,8,128]{3,1,2,0:T(8,128)S(1)} fusion(bf16[2048,1024]{1,0:T(8,128)(2,1)} %param.28, bf16[128,2048]{1,0:T(8,128)(2,1)} %scatter_fusion, f32[2048]{0:T(1024)S(1)} %copy-done.16, f32[128]{0:T(128)S(1)} %add_rsqrt_fusion.3), kind=kOutput, calls=%fused_computation.55 | convolution fusion | flops 537919488 | bytes 5251584 | tf_op jit(solution)/shard_map/dot_general | solution.py:39
  48.7 0.8 copy-done.2
  49.9 2.0 broadcast_multiply_fusion
  51.9 1.6 multiply_reduce_fusion.3
  54.1 1.4 subtract_convert_fusion
  55.5 0.9 multiply_reduce_fusion.1
  56.5 2.5 gather_fusion.2
  58.9 0.6 gather_fusion.4
  59.5 0.9 copy.124
  60.4 1.6 fusion.42
  62.0 0.7 copy.106
  62.7 7.4 %select_reduce_fusion.2 = (f32[368,8]{1,0:T(8,128)S(1)}, f32[368,8,64]{2,1,0:T(8,128)}) fusion(pred[368,64]{1,0:T(8,128)(4,1)S(1)} %fusion.65, bf16[368,1,64,128]{3,2,1,0:T(8,128)(2,1)} %param.24, bf16[368,8,128]{2,1,0:T(8,128)(2,1)} %gather_fusion.2, pred[368]{0:T(512)(128)(4,1)S(1)} %copy-done.21), kind=kOutput, calls=%fused_computation.48 | convolution fusion | flops 49173632 | bytes 7572336 | tf_op jit(solution)/shard_map/pgh,pth->pgt/dot_general | solution.py:84
  70.6 1.6 select_reduce_fusion.5
  72.3 0.6 fusion.91
  73.5 0.7 gather_fusion.7
  74.2 1.2 gather_fusion.6
  75.5 0.9 broadcast_select_fusion.4
  76.3 0.8 broadcast_select_fusion.2
  77.1 2.3 fusion.40
  79.7 3.8 %fusion.51 = f32[368,8,128]{2,1,0:T(8,128)S(1)} fusion(f32[368,8,64]{2,1,0:T(8,128)S(1)} %copy-done.1, f32[368,8]{1,0:T(8,128)S(1)} %broadcast_select_fusion.2, pred[368,64]{1,0:T(8,128)(4,1)S(1)} %copy-done.6, bf16[368,1,64,128]{3,2,1,0:T(8,128)(2,1)} %param.25), kind=kOutput, calls=%fused_computation.70 | convolution fusion | flops 48988160 | bytes 8325632 | tf_op jit(solution)/shard_map/pgt,pth->pgh/dot_general | solution.py:106
  83.5 1.3 fusion.78
  85.6 1.6 fusion.35
  87.1 0.6 fusion.39
  87.8 1.5 convolution_convert_fusion.1
  90.6 30.8 %all-gather.3.cloned.1.call-done = bf16[512,2048]{1,0:T(8,128)(2,1)} async-done(((bf16[128,2048]{1,0:T(8,128)(2,1)}), bf16[512,2048]{1,0:T(8,128)(2,1)}) %all-gather.3.cloned.1.call-update) | async-done | bytes 2097168 | tf_op jit(solution)/shard_map/all_gather | solution.py:195
  121.4 2.9 %reduce_sum.125 = bf16[128,2048]{1,0:T(8,128)(2,1)} reduce(bf16[4,128,2048]{2,1,0:T(8,128)(2,1)} %bitcast.179, bf16[]{:T(256)} %constant.231.clone.1), dimensions={0}, to_apply=%region_16.19 | reduce | flops 786432 | bytes 2621442 | tf_op jit(solution)/shard_map/reduce_sum | solution.py:194
  124.3 1.1 fusion.60
  125.5 2.1 convolution_convert_fusion
  127.6 4.1 %reshape.604 = bf16[128,1,4,2048]{3,2,0,1:T(4,128)(2,1)} reshape(bf16[512,2048]{1,0:T(8,128)(2,1)} %convolution_convert_fusion) | data formatting | bytes 4194304 | tf_op jit(solution)/shard_map/reshape | solution.py:222
  131.7 38.9 %all_to_all.10 = bf16[128,1,4,2048]{3,2,1,0:T(4,128)(2,1)S(1)} all-to-all(bf16[128,1,4,2048]{3,2,1,0:T(4,128)(2,1)} %bitcast.172), channel_id=1, replica_groups=mesh['req'=32,'kv'=4] {'req','kv'}, dimensions={0} | all-to-all | bytes 4194304 | tf_op jit(solution)/shard_map/all_to_all | solution.py:223
  170.6 1.3 copy-done.4
  171.9 4.8 %fusion.4 = f32[128,4,768]{2,0,1:T(8,128)} fusion(bf16[1,2048,768]{2,1,0:T(8,128)(2,1)S(1)} %copy-done.28, bf16[128,1,4,2048]{3,2,1,0:T(4,128)(2,1)S(1)} %all_to_all.10), kind=kOutput, calls=%fused_computation.19 | convolution fusion | flops 1610612736 | bytes 6815744 | tf_op jit(solution)/shard_map/sexd,edf->sexf/dot_general | solution.py:224
  176.7 9.9 %fusion.12 = bf16[128,1,4,2048]{3,0,2,1:T(8,128)(2,1)} fusion(bf16[1,768,2048]{2,1,0:T(8,128)(2,1)S(1)} %copy-done, bf16[1,2048,768]{2,1,0:T(8,128)(2,1)} %param.36, bf16[128,1,4,2048]{3,2,1,0:T(4,128)(2,1)} %copy-done.4, f32[128,4,768]{2,0,1:T(8,128)} %fusion.4), kind=kOutput, calls=%fused_computation.28 | convolution fusion | flops 3224633344 | bytes 12058624 | tf_op jit(solution)/shard_map/sexf,efd->sexd/dot_general | solution.py:228
  186.5 4.5 %copy.119 = bf16[128,1,4,2048]{3,2,1,0:T(4,128)(2,1)} copy(bf16[128,1,4,2048]{3,0,2,1:T(8,128)(2,1)} %fusion.12) | data formatting | bytes 4194304 | tf_op jit(solution)/shard_map/convert_element_type | solution.py:228
  191.0 5.1 %all-to-all-start.1 = ((bf16[128,1,4,2048]{3,2,1,0:T(4,128)(2,1)}), bf16[128,1,4,2048]{3,2,1,0:T(4,128)(2,1)}, u32[]{:S(2)}, u32[]{:S(2)}) async-start(bf16[128,1,4,2048]{3,2,1,0:T(4,128)(2,1)} %copy.119), calls=%async_computation.1 | async-start | bytes 4194304 | tf_op jit(solution)/shard_map/all_to_all | solution.py:227
  196.4 29.8 %all-to-all-done.1 = bf16[128,1,4,2048]{3,2,1,0:T(4,128)(2,1)} async-done(((bf16[128,1,4,2048]{3,2,1,0:T(4,128)(2,1)}), bf16[128,1,4,2048]{3,2,1,0:T(4,128)(2,1)}, u32[]{:S(2)}, u32[]{:S(2)}) %all-to-all-start.1) | async-done | bytes 2097184 | tf_op jit(solution)/shard_map/all_to_all | solution.py:227
  226.2 4.0 %reshape.610 = bf16[512,2048]{1,0:T(8,128)(2,1)} reshape(bf16[128,1,4,2048]{3,2,1,0:T(4,128)(2,1)} %all-to-all-done.1) | data formatting | bytes 4194304 | tf_op jit(solution)/shard_map/reshape | solution.py:236
  230.2 5.2 %gather_fusion.8 = bf16[256,2048]{1,0:T(8,128)(2,1)} fusion(bf16[512,2048]{1,0:T(8,128)(2,1)} %reshape.610, s32[1024]{0:T(1024)S(1)} %pad_clamp_fusion), kind=kCustom, calls=%fused_computation.12 | custom fusion | bytes 2098176 | tf_op jit(solution)/shard_map/jit(_take)/gather | solution.py:236
  235.4 2.9 %multiply_reduce_fusion = f32[32,2048]{1,0:T(8,128)S(1)} fusion(bf16[256,2048]{1,0:T(8,128)(2,1)} %gather_fusion.8, f32[32,8]{1,0:T(8,128)S(1)} %copy.111, pred[32,8]{1,0:T(8,128)(4,1)S(1)} %get-tuple-element.9), kind=kLoop, calls=%fused_computation.32 | loop fusion | flops 2031616 | bytes 1312000 | tf_op jit(solution)/shard_map/reduce_sum | solution.py:240
  238.3 0.7 fusion.63
  239.0 1.9 copy.167
  240.9 1.9 copy.168
  (138 shorter events, 7.0 us)
Async XLA Ops:
  7.2 169.5 %copy-start = (bf16[1,768,2048]{2,1,0:T(8,128)(2,1)S(1)}, bf16[1,768,2048]{2,1,0:T(8,128)(2,1)}, u32[]{:S(2)}) copy-start(bf16[1,768,2048]{2,1,0:T(8,128)(2,1)} %param.37) | copy-start | bytes 9437188
  7.2 114.2 %all-gather.3.cloned.1.call-start = ((), (), s32[]{:S(2)}) async-start(), calls=%async_computation.2 | async-start | bytes 2621440 | tf_op jit(solution)/shard_map/all_gather | solution.py:195
  13.5 28.2 %collective-permute-start = (bf16[2,2048]{1,0:T(2,128)(2,1)S(1)}, bf16[2,2048]{1,0:T(2,128)(2,1)S(1)}, u32[]{:S(2)}, u32[]{:S(2)}) collective-permute-start(bf16[2,2048]{1,0:T(2,128)(2,1)S(1)} %broadcast_select_fusion.3), channel_id=1, source_target_pairs={{0,64},{4,68},{8,72},{12,76},{16,80},{20,84},{24,88},{28,92},{32,9... | collective-permute-start | bytes 24584 | tf_op jit(solution)/shard_map/ppermute | solution.py:13
  27.1 5.7 %copy-start.9 = (s32[128,16]{0,1:T(8,128)S(1)}, s32[128,16]{0,1:T(8,128)}, u32[]{:S(2)}) copy-start(s32[128,16]{0,1:T(8,128)} %param.23) | copy-start | bytes 24580
  29.8 40.8 %collective-permute-start.1 = (bf16[2,1024,128]{2,1,0:T(8,128)(2,1)}, bf16[2,1024,128]{2,1,0:T(8,128)(2,1)}, u32[]{:S(2)}, u32[]{:S(2)}) collective-permute-start(bf16[2,1024,128]{2,1,0:T(8,128)(2,1)} %get-tuple-element.33), channel_id=1, source_target_pairs={{0,64},{4,68},{8,72},{12,76},{16,80},{20,84},{24,88},{28,92},{32,9... | collective-permute-start | bytes 1572872 | tf_op jit(solution)/shard_map/ppermute | solution.py:13
  29.9 53.7 %collective-permute-start.2 = (bf16[2,1024,128]{2,1,0:T(8,128)(2,1)}, bf16[2,1024,128]{2,1,0:T(8,128)(2,1)}, u32[]{:S(2)}, u32[]{:S(2)}) collective-permute-start(bf16[2,1024,128]{2,1,0:T(8,128)(2,1)} %get-tuple-element.32), channel_id=1, source_target_pairs={{0,64},{4,68},{8,72},{12,76},{16,80},{20,84},{24,88},{28,92},{32,9... | collective-permute-start | bytes 1572872 | tf_op jit(solution)/shard_map/ppermute | solution.py:13
  34.5 6.2 %copy-start.25 = (s32[32]{0:T(128)}, s32[32]{0:T(128)S(1)}, u32[]{:S(2)}) copy-start(s32[32]{0:T(128)S(1)} %eq.110) | copy-start | bytes 388
  35.1 10.3 %copy-start.16 = (f32[2048]{0:T(1024)S(1)}, f32[2048]{0:T(1024)}, u32[]{:S(2)}) copy-start(f32[2048]{0:T(1024)} %param.27) | copy-start | bytes 24580
  35.7 20.7 %copy-start.10 = (s32[1024]{0:T(1024)}, s32[1024]{0:T(1024)S(1)}, u32[]{:S(2)}) copy-start(s32[1024]{0:T(1024)S(1)} %pad_clamp_fusion.4) | copy-start | bytes 12292
  39.1 9.5 %copy-start.22 = (pred[368]{0:T(512)(128)(4,1)}, pred[368]{0:T(512)(128)(4,1)S(1)}, u32[]{:S(2)}) copy-start(pred[368]{0:T(512)(128)(4,1)S(1)} %not_and_fusion) | copy-start | bytes 1108
  39.9 19.1 %copy-start.19 = (s32[1024]{0:T(1024)}, s32[1024]{0:T(1024)S(1)}, u32[]{:S(2)}) copy-start(s32[1024]{0:T(1024)S(1)} %pad_clamp_fusion.3) | copy-start | bytes 12292
  41.5 21.2 %copy-start.5 = (pred[368,64]{1,0:T(8,128)(4,1)}, pred[368,64]{1,0:T(8,128)(4,1)S(1)}, u32[]{:S(2)}) copy-start(pred[368,64]{1,0:T(8,128)(4,1)S(1)} %fusion.65) | copy-start | bytes 70660
  45.4 6.5 %copy-start.27 = (f32[128]{0:T(128)}, f32[128]{0:T(128)S(1)}, u32[]{:S(2)}) copy-start(f32[128]{0:T(128)S(1)} %add_rsqrt_fusion.3) | copy-start | bytes 1540
  48.7 0.8 copy-start.2
  55.5 7.2 %copy-start.21 = (pred[368]{0:T(512)(128)(4,1)S(1)}, pred[368]{0:T(512)(128)(4,1)}, u32[]{:S(2)}) copy-start(pred[368]{0:T(512)(128)(4,1)} %get-tuple-element.18) | copy-start | bytes 1108
  60.4 11.9 %copy-start.12 = (f32[128,8]{0,1:T(8,128)}, f32[128,8]{0,1:T(8,128)S(1)}, u32[]{:S(2)}) copy-start(f32[128,8]{0,1:T(8,128)S(1)} %copy.124) | copy-start | bytes 12292
  62.7 7.4 %copy-start.8 = (pred[368,128]{1,0:T(8,128)(4,1)S(1)}, pred[368,128]{1,0:T(8,128)(4,1)}, u32[]{:S(2)}) copy-start(pred[368,128]{1,0:T(8,128)(4,1)} %fusion.64) | copy-start | bytes 141316
  62.7 7.9 %copy-start.20 = (pred[32]{0:T(512)(128)(4,1)S(1)}, pred[32]{0:T(512)(128)(4,1)}, u32[]{:S(2)}) copy-start(pred[32]{0:T(512)(128)(4,1)} %get-tuple-element.20) | copy-start | bytes 100
  72.9 0.6 copy-start.14
  75.4 4.2 %copy-start.1 = (f32[368,8,64]{2,1,0:T(8,128)S(1)}, f32[368,8,64]{2,1,0:T(8,128)}, u32[]{:S(2)}) copy-start(f32[368,8,64]{2,1,0:T(8,128)} %get-tuple-element.45) | copy-start | bytes 2260996
  75.5 4.2 %copy-start.6 = (pred[368,64]{1,0:T(8,128)(4,1)S(1)}, pred[368,64]{1,0:T(8,128)(4,1)}, u32[]{:S(2)}) copy-start(pred[368,64]{1,0:T(8,128)(4,1)} %copy-done.5) | copy-start | bytes 70660
  79.6 5.3 %copy-start.13 = (f32[128,8]{0,1:T(8,128)S(1)}, f32[128,8]{0,1:T(8,128)}, u32[]{:S(2)}) copy-start(f32[128,8]{0,1:T(8,128)} %copy-done.12) | copy-start | bytes 12292
  79.6 5.3 %copy-start.15 = (f32[128,8]{0,1:T(8,128)S(1)}, f32[128,8]{0,1:T(8,128)}, u32[]{:S(2)}) copy-start(f32[128,8]{0,1:T(8,128)} %copy-done.14) | copy-start | bytes 12292
  79.6 5.3 %copy-start.23 = (pred[368]{0:T(512)(128)(4,1)S(1)}, pred[368]{0:T(512)(128)(4,1)}, u32[]{:S(2)}) copy-start(pred[368]{0:T(512)(128)(4,1)} %copy-done.22) | copy-start | bytes 1108
  79.7 5.7 %copy-start.18 = (bf16[128,8]{0,1:T(8,128)(2,1)S(1)}, bf16[128,8]{0,1:T(8,128)(2,1)}, u32[]{:S(2)}) copy-start(bf16[128,8]{0,1:T(8,128)(2,1)} %get-tuple-element.13) | copy-start | bytes 6148
  79.7 5.7 %copy-start.26 = (s32[32]{0:T(128)S(1)}, s32[32]{0:T(128)}, u32[]{:S(2)}) copy-start(s32[32]{0:T(128)} %copy-done.25) | copy-start | bytes 388
  79.7 5.9 %copy-start.7 = (f32[128,128]{0,1:T(8,128)S(1)}, f32[128,128]{0,1:T(8,128)}, u32[]{:S(2)}) copy-start(f32[128,128]{0,1:T(8,128)} %copy.106) | copy-start | bytes 196612
  85.4 2.4 copy-start.3
  87.8 1.6 copy-start.24
  89.4 36.1 %copy-start.17 = (f32[2048]{0:T(1024)S(1)}, f32[2048]{0:T(1024)}, u32[]{:S(2)}) copy-start(f32[2048]{0:T(1024)} %param.32) | copy-start | bytes 24580
  131.7 40.2 %copy-start.28 = (bf16[1,2048,768]{2,1,0:T(8,128)(2,1)S(1)}, bf16[1,2048,768]{2,1,0:T(8,128)(2,1)}, u32[]{:S(2)}) copy-start(bf16[1,2048,768]{2,1,0:T(8,128)(2,1)} %param.35) | copy-start | bytes 9437188
  170.6 1.3 copy-start.4
  191.0 5.2 %copy-start.11 = (f32[32,8]{0,1:T(8,128)S(1)}, f32[32,8]{0,1:T(8,128)}, u32[]{:S(2)}) copy-start(f32[32,8]{0,1:T(8,128)} %param.34) | copy-start | bytes 3076
  191.0 35.2 %all-to-all-start.1 = ((bf16[128,1,4,2048]{3,2,1,0:T(4,128)(2,1)}), bf16[128,1,4,2048]{3,2,1,0:T(4,128)(2,1)}, u32[]{:S(2)}, u32[]{:S(2)}) async-start(bf16[128,1,4,2048]{3,2,1,0:T(4,128)(2,1)} %copy.119), calls=%async_computation.1 | async-start | bytes 4194304 | tf_op jit(solution)/shard_map/all_to_all | solution.py:227
Sparse Core Ops, SparseCore 0:
  89.5 31.9 all-gather.2
